TPU v7x, 32 devices: a whole 2x2x4 slice. The times are simulated.
32 devices in a mesh: tile: 4 (over x, core), blk: 8 (over z, y).
Axes of the slice: x: 2, y: 2, z: 4, core: 2. Of those that a mesh axis runs over, the one named last changes fastest.
Arguments:
- tokens: bfloat16 [32768, 384], P(('tile', 'blk')), may hold values from -52 to 52
- ln_gain: float32 [384], replicated, may hold values from 0.1 to 1.9
- route: int32 [32768, 2], P(('tile', 'blk')), may hold values from 0 to 15, all different within a row; in each aligned block of 1024 rows (0 to 1023, 1024 to 2047, ...) at most 192 rows name the same one
- gates: float32 [32768, 2], P(('tile', 'blk')), may hold values from 0.1 to 1
- w_gate: bfloat16 [16, 384, 1024], P('tile', 'blk'), may hold values from -0.3125 to 0.3125
- w_up: bfloat16 [16, 384, 1024], P('tile', 'blk'), may hold values from -0.3125 to 0.3125
- w_down: bfloat16 [16, 1024, 384], P('tile', 'blk'), may hold values from -0.1875 to 0.1875
- d_mixed: bfloat16 [32768, 384], P(('tile', 'blk')), may hold values from -6 to 6
Outputs:
- mixed: bfloat16 [32768, 384], P(('tile', 'blk'))
- grad_gates: float32 [32768, 2], P(('tile', 'blk'))
- grad_tokens: bfloat16 [32768, 384], P(('tile', 'blk'))
- grad_w_gate: float32 [16, 384, 1024], P('tile', 'blk')
- grad_w_up: float32 [16, 384, 1024], P('tile', 'blk')
- grad_w_down: float32 [16, 1024, 384], P('tile', 'blk')
Inputs may be any that keep to these rules, and one draw needn't show every extreme that they name: `route`: each row names 2 different experts; within the rows of one device no expert is named more than 192 times, a bound that some block reaches.
All inputs are finite; a program needn't handle non-finite values.
Results may differ from a plain program's by a relative error of at most 0.014.
Values may be sent and summed in bfloat16 or wider, within the bound.
A program may use at most 192 MiB of HBM per device.

v0:
```python
import jax
import jax.numpy as jnp
from jax import lax
from jax.sharding import PartitionSpec as P


def layer_norm(values, ln_gain):
    centre = jnp.mean(values, axis=-1, keepdims=True)
    centred = values - centre
    spread = jnp.mean(centred * centred, axis=-1, keepdims=True)
    return values * lax.rsqrt(spread + 1e-05) * ln_gain


def expert_forward(inputs_rows, weight_gate, weight_up, weight_down):
    gate_pre = jnp.einsum(
        "erd,edh->erh", inputs_rows, weight_gate, preferred_element_type=jnp.float32
    )
    up_pre = jnp.einsum("erd,edh->erh", inputs_rows, weight_up, preferred_element_type=jnp.float32)
    sigma_gate = jax.nn.sigmoid(gate_pre)
    hidden_act = (gate_pre * sigma_gate * up_pre).astype(jnp.bfloat16)
    expert_rows = jnp.einsum(
        "erh,ehd->erd", hidden_act, weight_down, preferred_element_type=jnp.float32
    )
    return (expert_rows.astype(jnp.bfloat16), gate_pre, up_pre, hidden_act)


def expert_backward(
    inputs_rows, d_rows, gate_pre, up_pre, hidden_act, weight_gate, weight_up, weight_down
):
    d_act = jnp.einsum("erd,ehd->erh", d_rows, weight_down, preferred_element_type=jnp.float32)
    sigma_gate = jax.nn.sigmoid(gate_pre)
    d_gate = (d_act * up_pre * sigma_gate * (1.0 + gate_pre * (1.0 - sigma_gate))).astype(
        jnp.bfloat16
    )
    d_up = (d_act * gate_pre * sigma_gate).astype(jnp.bfloat16)
    d_in = jnp.einsum(
        "erh,edh->erd", d_gate, weight_gate, preferred_element_type=jnp.float32
    ) + jnp.einsum("erh,edh->erd", d_up, weight_up, preferred_element_type=jnp.float32)
    grad_gate = jnp.einsum("erd,erh->edh", inputs_rows, d_gate, preferred_element_type=jnp.float32)
    grad_up = jnp.einsum("erd,erh->edh", inputs_rows, d_up, preferred_element_type=jnp.float32)
    grad_down = jnp.einsum("erh,erd->ehd", hidden_act, d_rows, preferred_element_type=jnp.float32)
    return (d_in.astype(jnp.bfloat16), grad_gate, grad_up, grad_down)


def on_device(tokens, ln_gain, route, gates, w_gate, w_up, w_down, d_mixed):
    tok_rows, features = tokens.shape
    top_picks = route.shape[1]
    per_tile = w_gate.shape[0]
    tile_count = lax.axis_size("tile")
    experts_all = per_tile * tile_count
    capacity = max(2, 3 * tok_rows * top_picks // (2 * experts_all))
    tokens_wide = tokens.astype(jnp.float32)
    normed = layer_norm(tokens_wide, ln_gain).astype(jnp.bfloat16)
    flat_route = route.reshape(-1)
    onehot = (flat_route[:, None] == lax.iota(jnp.int32, experts_all)[None, :]).astype(jnp.int32)
    slot_rank = jnp.sum((jnp.cumsum(onehot, axis=0) - 1) * onehot, axis=1)
    slot_index = flat_route * capacity + slot_rank

    def pack_slots(values):
        blank = jnp.zeros((experts_all * capacity, features), jnp.bfloat16)
        return blank.at[slot_index].set(values).reshape(tile_count, per_tile, capacity, features)

    def to_experts(packed):
        arrived = lax.all_to_all(packed, "tile", split_axis=0, concat_axis=2, tiled=True)[0]
        return arrived

    def from_experts(results):
        returned = lax.all_to_all(results[None], "tile", split_axis=2, concat_axis=0, tiled=True)
        picked = returned.reshape(experts_all * capacity, features)[slot_index]
        return picked.reshape(tok_rows, top_picks, features).astype(jnp.float32)

    weight_gate, weight_up, weight_down = (
        lax.all_gather(w_gate, "blk", axis=1, tiled=True),
        lax.all_gather(w_up, "blk", axis=1, tiled=True),
        lax.all_gather(w_down, "blk", axis=1, tiled=True),
    )
    inputs_rows = to_experts(pack_slots(jnp.repeat(normed, top_picks, axis=0)))
    expert_rows, gate_pre, up_pre, hidden_act = expert_forward(
        inputs_rows, weight_gate, weight_up, weight_down
    )
    expert_out = from_experts(expert_rows)
    mixed = jnp.sum(gates[:, :, None] * expert_out, axis=1).astype(jnp.bfloat16)
    d_wide = d_mixed.astype(jnp.float32)
    grad_gates = jnp.sum(d_wide[:, None, :] * expert_out, axis=-1)
    d_out = (
        (gates[:, :, None] * d_wide[:, None, :])
        .astype(jnp.bfloat16)
        .reshape(tok_rows * top_picks, features)
    )
    d_rows = to_experts(pack_slots(d_out))
    d_in, grad_gate, grad_up, grad_down = expert_backward(
        inputs_rows, d_rows, gate_pre, up_pre, hidden_act, weight_gate, weight_up, weight_down
    )
    d_normed = jnp.sum(from_experts(d_in), axis=1)

    def normalize(values):
        return layer_norm(values, ln_gain)

    unused, pullback = jax.vjp(normalize, tokens_wide)
    grad_tokens = pullback(d_normed)[0].astype(jnp.bfloat16)
    total_gate, total_up, total_down = (
        lax.psum_scatter(
            grad_gate.astype(jnp.bfloat16), "blk", scatter_dimension=1, tiled=True
        ).astype(jnp.float32),
        lax.psum_scatter(
            grad_up.astype(jnp.bfloat16), "blk", scatter_dimension=1, tiled=True
        ).astype(jnp.float32),
        lax.psum_scatter(
            grad_down.astype(jnp.bfloat16), "blk", scatter_dimension=1, tiled=True
        ).astype(jnp.float32),
    )
    return (mixed, grad_gates, grad_tokens, total_gate, total_up, total_down)


def solution(mesh):
    placed = (
        P(("tile", "blk"), None),
        P(),
        P(("tile", "blk"), None),
        P(("tile", "blk"), None),
        P("tile", "blk", None),
        P("tile", "blk", None),
        P("tile", "blk", None),
        P(("tile", "blk"), None),
    )
    return jax.shard_map(
        on_device,
        mesh=mesh,
        in_specs=placed,
        out_specs=(
            P(("tile", "blk"), None),
            P(("tile", "blk"), None),
            P(("tile", "blk"), None),
            P("tile", "blk", None),
            P("tile", "blk", None),
            P("tile", "blk", None),
        ),
        check_vma=False,
    )
```

profile of v0, /device:TPU:0, one launch (start us, length us, event | category | flops | bytes accessed | tf_op | source)
XLA Modules:
  0.0 456.1 jit_solution(16825820951956494859)
XLA Ops:
  20.1 11.6 %scatter_custom_fusion = bf16[3072,384]{1,0:T(8,128)(2,1)} fusion(s32[2048]{0:T(1024)S(1)} %bitcast.70, bf16[2048,384]{1,0:T(8,128)(2,1)} %reshape.153, bf16[]{:T(256)} %constant.10.clone.1), kind=kCustom, calls=%fused_computation.35 | custom fusion | bytes 2359808 | tf_op jit(solution)/shard_map/scatter | solution.py:61
  42.2 5.4 %mul.150 = f32[2048,384]{1,0:T(8,128)} reshape(f32[1024,2,384]{2,1,0:T(2,128)} %mul.146) | data formatting | bytes 6291456 | tf_op jit(solution)/shard_map/mul | solution.py:84
  47.6 12.6 %scatter_custom_fusion.1 = bf16[3072,384]{1,0:T(8,128)(2,1)} fusion(s32[2048]{0:T(1024)S(1)} %bitcast.71, f32[2048,384]{1,0:T(8,128)} %mul.150, f32[2048]{0:T(1024)S(1)} %mul.148, bf16[]{:T(256)} %constant.10.clone.1), kind=kCustom, calls=%fused_computation.32 | custom fusion | flops 1572864 | bytes 5513218 | tf_op jit(solution)/shard_map/scatter | solution.py:61
  72.9 26.3 %all-to-all-done.2 = bf16[4,4,192,384]{3,2,1,0:T(8,128)(2,1)} async-done(((bf16[4,4,192,384]{3,2,1,0:T(8,128)(2,1)}), bf16[4,4,192,384]{3,2,1,0:T(8,128)(2,1)}, u32[]{:S(2)}, u32[]{:S(2)}) %all-to-all-start.2) | async-done | bytes 2359328 | tf_op jit(solution)/shard_map/all_to_all | solution.py:64
  102.6 8.7 %fusion.21 = f32[4,768,1024]{2,1,0:T(8,128)} fusion(bf16[4,768,384]{2,1,0:T(8,128)(2,1)S(1)} %bitcast.58, bf16[4,384,1024]{2,1,0:T(8,128)(2,1)} %all-gather.4.cloned.1.call-done), kind=kOutput, calls=%fused_computation.53 | convolution fusion | flops 2415919104 | bytes 18087936 | tf_op jit(solution)/shard_map/erd,edh->erh/dot_general | solution.py:15
  111.3 22.6 %all-gather.6.cloned.1.call-done = bf16[4,384,1024]{2,1,0:T(8,128)(2,1)} async-done(((bf16[4,48,1024]{2,1,0:T(8,128)(2,1)}), bf16[4,384,1024]{2,1,0:T(8,128)(2,1)}) %all-gather.6.cloned.1.call-update) | async-done | bytes 3145744 | tf_op jit(solution)/shard_map/all_gather | solution.py:74
  133.9 8.3 %fusion.22 = f32[4,768,1024]{2,1,0:T(8,128)} fusion(bf16[4,768,384]{2,1,0:T(8,128)(2,1)S(1)} %bitcast.59, bf16[4,384,1024]{2,1,0:T(8,128)(2,1)} %all-gather.6.cloned.1.call-done), kind=kOutput, calls=%fused_computation.54 | convolution fusion | flops 2415919104 | bytes 18087936 | tf_op jit(solution)/shard_map/erd,edh->erh/dot_general | solution.py:18
  142.2 52.6 %all-gather.8.cloned.1.call-done = bf16[4,1024,384]{2,1,0:T(8,128)(2,1)} async-done(((bf16[4,128,384]{2,1,0:T(8,128)(2,1)}), bf16[4,1024,384]{2,1,0:T(8,128)(2,1)}) %all-gather.8.cloned.1.call-update) | async-done | bytes 3145744 | tf_op jit(solution)/shard_map/all_gather | solution.py:75
  194.8 18.0 %multiply_convert_fusion = (bf16[4,768,1024]{2,1,0:T(8,128)(2,1)}, bf16[4,768,1024]{2,1,0:T(8,128)(2,1)}, bf16[4,768,1024]{2,1,0:T(8,128)(2,1)}) fusion(f32[4,768,1024]{2,1,0:T(8,128)} %fusion.21, f32[4,768,1024]{2,1,0:T(8,128)} %fusion.22, bf16[4,768,384]{2,1,0:T(8,128)(2,1)} %bitcast.66, bf16[4,1024,384]{2,1,0:T(8,128)(2,1)} %all-gather.8.cloned.1.call-done), kind=kOutput, calls=%fused_computation.4 | convolution fusion | flops 2466250752 | bytes 49545216 | tf_op jit(solution)/shard_map/erd,ehd->erh/dot_general | solution.py:30
  212.8 7.1 %convolution_convert_fusion.2 = bf16[4,384,1024]{2,1,0:T(8,128)(2,1)} fusion(bf16[4,768,384]{2,1,0:T(8,128)(2,1)S(1)} %bitcast.60, bf16[4,768,1024]{2,1,0:T(8,128)(2,1)} %get-tuple-element.15), kind=kOutput, calls=%fused_computation.20 | convolution fusion | flops 2417491968 | bytes 11796480 | tf_op jit(solution)/shard_map/erd,erh->edh/dot_general | solution.py:39
  220.5 7.1 %convolution_convert_fusion.1 = bf16[4,384,1024]{2,1,0:T(8,128)(2,1)} fusion(bf16[4,768,384]{2,1,0:T(8,128)(2,1)S(1)} %bitcast.61, bf16[4,768,1024]{2,1,0:T(8,128)(2,1)} %get-tuple-element.14), kind=kOutput, calls=%fused_computation.19 | convolution fusion | flops 2417491968 | bytes 11796480 | tf_op jit(solution)/shard_map/erd,erh->edh/dot_general | solution.py:40
  229.3 8.0 %convolution_convert_fusion = bf16[4,1024,384]{2,1,0:T(8,128)(2,1)} fusion(bf16[4,768,1024]{2,1,0:T(8,128)(2,1)} %get-tuple-element.16, bf16[4,768,384]{2,1,0:T(8,128)(2,1)S(1)} %bitcast.67), kind=kOutput, calls=%fused_computation.18 | convolution fusion | flops 2417491968 | bytes 11796480 | tf_op jit(solution)/shard_map/erh,erd->ehd/dot_general | solution.py:41
  237.3 6.7 %fusion.23 = f32[4,768,384]{2,1,0:T(8,128)S(1)} fusion(bf16[4,768,1024]{2,1,0:T(8,128)(2,1)} %get-tuple-element.15, bf16[4,384,1024]{2,1,0:T(8,128)(2,1)} %all-gather.4.cloned.1.call-done), kind=kOutput, calls=%fused_computation.55 | convolution fusion | flops 2415919104 | bytes 14155776 | tf_op jit(solution)/shard_map/erh,edh->erd/dot_general | solution.py:36
  254.7 7.2 %convert_bitcast_fusion = bf16[1,4,768,384]{3,2,1,0:T(8,128)(2,1)S(1)} fusion(bf16[4,768,1024]{2,1,0:T(8,128)(2,1)} %get-tuple-element.16, bf16[4,1024,384]{2,1,0:T(8,128)(2,1)} %all-gather.8.cloned.1.call-done), kind=kOutput, calls=%fused_computation.17 | convolution fusion | flops 2417098752 | bytes 11796480 | tf_op jit(solution)/shard_map/erh,ehd->erd/dot_general | solution.py:21
  265.1 18.0 %all-to-all-done.3 = bf16[1,4,768,384]{3,1,0,2:T(4,128)(2,1)S(1)} async-done(((bf16[1,4,768,384]{3,1,0,2:T(4,128)(2,1)}), bf16[1,4,768,384]{3,1,0,2:T(4,128)(2,1)S(1)}, u32[]{:S(2)}, u32[]{:S(2)}) %all-to-all-start.3) | async-done | bytes 2359328 | tf_op jit(solution)/shard_map/all_to_all | solution.py:68
  292.2 9.0 %gather_fusion.1 = bf16[2048,384]{1,0:T(8,128)(2,1)} fusion(bf16[3072,384]{1,0:T(8,128)(2,1)S(1)} %bitcast.57, s32[2048]{0:T(1024)S(1)} %broadcast_clamp_fusion), kind=kCustom, calls=%fused_computation.1 | custom fusion | bytes 3153920 | tf_op jit(solution)/shard_map/gather | solution.py:69
  301.2 4.9 %reshape.132 = f32[1024,2,384]{2,1,0:T(2,128)} reshape(bf16[2048,384]{1,0:T(8,128)(2,1)} %gather_fusion.1) | data formatting | bytes 4718592 | tf_op jit(solution)/shard_map/convert_element_type | solution.py:70
  306.1 11.6 %all-to-all-done.1 = bf16[1,4,768,384]{3,1,0,2:T(4,128)(2,1)} async-done(((bf16[1,4,768,384]{3,1,0,2:T(4,128)(2,1)}), bf16[1,4,768,384]{3,1,0,2:T(4,128)(2,1)}, u32[]{:S(2)}, u32[]{:S(2)}) %all-to-all-start.1) | async-done | bytes 2359328 | tf_op jit(solution)/shard_map/all_to_all | solution.py:68
  319.9 9.1 %gather_fusion = bf16[2048,384]{1,0:T(8,128)(2,1)} fusion(bf16[3072,384]{1,0:T(8,128)(2,1)S(1)} %bitcast.56, s32[2048]{0:T(1024)S(1)} %broadcast_clamp_fusion), kind=kCustom, calls=%fused_computation | custom fusion | bytes 3153920 | tf_op jit(solution)/shard_map/gather | solution.py:69
  328.9 5.0 %reshape.131 = f32[1024,2,384]{2,1,0:T(2,128)} reshape(bf16[2048,384]{1,0:T(8,128)(2,1)} %gather_fusion) | data formatting | bytes 4718592 | tf_op jit(solution)/shard_map/convert_element_type | solution.py:70
  334.0 10.1 %multiply_reduce_fusion = (f32[1024,2]{1,0:T(8,128)S(1)}, bf16[1024,384]{1,0:T(8,128)(2,1)}) fusion(f32[1024,2,384]{2,1,0:T(2,128)} %reshape.131, f32[1024,384]{1,0:T(8,128)S(1)} %copy-done.4, f32[1024,2]{1,0:T(8,128)S(1)} %copy-done.5), kind=kLoop, calls=%fused_computation.10 | loop fusion | flops 2750464 | bytes 5521408 | tf_op jit(solution)/shard_map/reduce_sum | solution.py:84
  344.9 5.7 %reduce_sum.96 = f32[1024,384]{1,0:T(8,128)S(1)} reduce(f32[1024,2,384]{2,1,0:T(2,128)} %reshape.132, f32[]{:T(128)} %constant.25.clone.1), dimensions={1}, to_apply=%region_9.10 | reduce | flops 393216 | bytes 4718596 | tf_op jit(solution)/shard_map/reduce_sum | solution.py:94
  355.0 15.0 %reduce-scatter.6.cloned.1.call-done = bf16[4,48,1024]{2,1,0:T(8,128)(2,1)} async-done(((bf16[4,384,1024]{2,1,0:T(8,128)(2,1)}), bf16[4,48,1024]{2,1,0:T(8,128)(2,1)}) %reduce-scatter.6.cloned.1.call-update) | async-done | bytes 393232 | tf_op jit(solution)/shard_map/reduce_scatter | solution.py:105
  372.0 75.1 %reduce-scatter.8.cloned.1.call-done = bf16[4,128,384]{2,1,0:T(8,128)(2,1)} async-done(((bf16[4,1024,384]{2,1,0:T(8,128)(2,1)}), bf16[4,128,384]{2,1,0:T(8,128)(2,1)}) %reduce-scatter.8.cloned.1.call-update) | async-done | bytes 393232 | tf_op jit(solution)/shard_map/reduce_scatter | solution.py:108
  (87 shorter events, 75.8 us)
Async XLA Ops:
  7.2 8.7 %copy-start = (bf16[1024,384]{1,0:T(8,128)(2,1)S(1)}, bf16[1024,384]{1,0:T(8,128)(2,1)}, u32[]{:S(2)}) copy-start(bf16[1024,384]{1,0:T(8,128)(2,1)} %param.8) | copy-start | bytes 2359300
  7.2 9.4 %copy-start.9 = (f32[384]{0:T(512)S(1)}, f32[384]{0:T(512)}, u32[]{:S(2)}) copy-start(f32[384]{0:T(512)} %param.9) | copy-start | bytes 4612
  7.2 95.4 %all-gather.4.cloned.1.call-start = ((), (), s32[]{:S(2)}) async-start(), calls=%async_computation.7 | async-start | bytes 3538944 | tf_op jit(solution)/shard_map/all_gather | solution.py:73
  7.9 126.0 %all-gather.6.cloned.1.call-start = ((), (), s32[]{:S(2)}) async-start(), calls=%async_computation.8 | async-start | bytes 3538944 | tf_op jit(solution)/shard_map/all_gather | solution.py:74
  8.7 186.1 %all-gather.8.cloned.1.call-start = ((), (), s32[]{:S(2)}) async-start(), calls=%async_computation.9 | async-start | bytes 3538944 | tf_op jit(solution)/shard_map/all_gather | solution.py:75
  10.3 6.5 %copy-start.8 = (s32[1024,2]{0,1:T(2,128)S(1)}, s32[1024,2]{0,1:T(2,128)}, u32[]{:S(2)}) copy-start(s32[1024,2]{0,1:T(2,128)} %param.10) | copy-start | bytes 24580
  31.7 4.5 copy-start.10
  31.7 33.1 %all-to-all-start = ((bf16[4,4,192,384]{3,2,1,0:T(8,128)(2,1)}), bf16[4,4,192,384]{3,2,1,0:T(8,128)(2,1)S(1)}, u32[]{:S(2)}, u32[]{:S(2)}) async-start(bf16[4,4,192,384]{3,2,1,0:T(8,128)(2,1)} %bitcast.65), calls=%async_computation | async-start | bytes 4718592 | tf_op jit(solution)/shard_map/all_to_all | solution.py:64
  64.8 1.4 copy-start.1
  66.2 33.0 %all-to-all-start.2 = ((bf16[4,4,192,384]{3,2,1,0:T(8,128)(2,1)}), bf16[4,4,192,384]{3,2,1,0:T(8,128)(2,1)}, u32[]{:S(2)}, u32[]{:S(2)}) async-start(bf16[4,4,192,384]{3,2,1,0:T(8,128)(2,1)} %bitcast.64), calls=%async_computation.2 | async-start | bytes 4718592 | tf_op jit(solution)/shard_map/all_to_all | solution.py:64
  70.7 282.4 %reduce-scatter.4.cloned.1.call-start = ((), (), s32[]{:S(2)}) async-start(), calls=%async_computation.10 | async-start | bytes 3538944 | tf_op jit(solution)/shard_map/reduce_scatter | solution.py:102
  219.9 150.1 %reduce-scatter.6.cloned.1.call-start = ((), (), s32[]{:S(2)}) async-start(), calls=%async_computation.11 | async-start | bytes 3538944 | tf_op jit(solution)/shard_map/reduce_scatter | solution.py:105
  227.6 1.7 copy-start.7
  227.6 219.5 %reduce-scatter.8.cloned.1.call-start = ((), (), s32[]{:S(2)}) async-start(), calls=%async_computation.12 | async-start | bytes 3538944 | tf_op jit(solution)/shard_map/reduce_scatter | solution.py:108
  237.2 6.7 %slice-start = ((s8[6291456]{0:T(1024)(128)(4,1)}), s8[2097152]{0:T(1024)(128)(4,1)S(1)}, s32[]{:S(2)}) async-start(s8[6291456]{0:T(1024)(128)(4,1)} %bitcast.74), calls=%async_computation.13 | async-start | bytes 4194304
  237.2 6.7 %copy-start.6 = (bf16[4,384,1024]{2,1,0:T(8,128)(2,1)S(1)}, bf16[4,384,1024]{2,1,0:T(8,128)(2,1)}, u32[]{:S(2)}) copy-start(bf16[4,384,1024]{2,1,0:T(8,128)(2,1)} %all-gather.6.cloned.1.call-done) | copy-start | bytes 9437188
  237.2 6.8 %slice-start.1 = ((s8[6291456]{0:T(1024)(128)(4,1)}), s8[4194304]{0:T(1024)(128)(4,1)S(1)}, s32[]{:S(2)}) async-start(s8[6291456]{0:T(1024)(128)(4,1)} %bitcast.74), calls=%async_computation.14 | async-start | bytes 8388608
  251.0 32.1 %all-to-all-start.3 = ((bf16[1,4,768,384]{3,1,0,2:T(4,128)(2,1)}), bf16[1,4,768,384]{3,1,0,2:T(4,128)(2,1)S(1)}, u32[]{:S(2)}, u32[]{:S(2)}) async-start(bf16[1,4,768,384]{3,1,0,2:T(4,128)(2,1)} %copy.41), calls=%async_computation.3 | async-start | bytes 4718592 | tf_op jit(solution)/shard_map/all_to_all | solution.py:68
  283.1 1.4 copy-start.2
  284.5 33.2 %all-to-all-start.1 = ((bf16[1,4,768,384]{3,1,0,2:T(4,128)(2,1)}), bf16[1,4,768,384]{3,1,0,2:T(4,128)(2,1)}, u32[]{:S(2)}, u32[]{:S(2)}) async-start(bf16[1,4,768,384]{3,1,0,2:T(4,128)(2,1)} %copy.37), calls=%async_computation.1 | async-start | bytes 4718592 | tf_op jit(solution)/shard_map/all_to_all | solution.py:68
  289.2 2.6 copy-start.3
  328.9 5.0 %copy-start.4 = (f32[1024,384]{1,0:T(8,128)S(1)}, f32[1024,384]{1,0:T(8,128)}, u32[]{:S(2)}) copy-start(f32[1024,384]{1,0:T(8,128)} %convert_element_type.81) | copy-start | bytes 4718596
  328.9 5.0 %copy-start.5 = (f32[1024,2]{1,0:T(8,128)S(1)}, f32[1024,2]{1,0:T(8,128)}, u32[]{:S(2)}) copy-start(f32[1024,2]{1,0:T(8,128)} %copy.32) | copy-start | bytes 24580
Sparse Core Ops, SparseCore 0:
  10.2 62.7 all-gather.3
  75.2 58.6 all-gather.5
  136.1 58.6 all-gather.7
  220.1 72.9 reduce-scatter.3
  296.5 73.4 reduce-scatter.5
  373.4 73.5 reduce-scatter.7
where the time goes:
time: 463 us; the launch traced here: 456 us
  waiting for transfers between devices  228 us (49%)
  local copies, waits for them, and re-layouts  75.3 us (16%)
  matrix products  74.9 us (16%)
  other arithmetic  45.1 us (10%)
  starting transfers between devices  18.2 us (4%)
  between operations  14.6 us (3%)
    reduce_scatter x1, waiting for transfers between devices, on_device(): lax.psum_scatter(grad_down.astype(jnp.bfloat16), 'blk', scatter_dimension...  75.1 us
    all_gather x1, waiting for transfers between devices, on_device(): lax.all_gather(w_down, 'blk', axis=1, tiled=True)  52.6 us
    all_to_all x2, waiting for transfers between devices, to_experts(): lax.all_to_all(packed, 'tile', split_axis=0, concat_axis=2, tiled=True)[0]  30.9 us
    all_to_all x2, waiting for transfers between devices, from_experts(): lax.all_to_all(results[None], 'tile', split_axis=2, concat_axis=0, tiled=...  29.6 us
    all_gather x1, waiting for transfers between devices, on_device(): lax.all_gather(w_up, 'blk', axis=1, tiled=True)  22.6 us
    gather x2, local copies, waits for them, and re-layouts, from_experts(): picked = returned.reshape(experts_all * capacity, features)[slot_index]  18.1 us
    dot_general x1, matrix products, expert_backward(): jnp.einsum('erd,ehd->erh', d_rows, weight_down, preferred_element_type=jn...  18 us
    reduce_scatter x1, waiting for transfers between devices, on_device(): lax.psum_scatter(grad_up.astype(jnp.bfloat16), 'blk', scatter_dimension=1...  15 us
  transfers between devices with their start and end apart: 10, of which 8 were waited for; matrix products, arithmetic and copies ran while one was open for 36% of the time, Pallas kernels for 0%

commit v1 on v0

--- a/solution.py
+++ b/solution.py
@@ -1,7 +1,17 @@
+import functools
 import jax
 import jax.numpy as jnp
 from jax import lax
 from jax.sharding import PartitionSpec as P
+
+
+def read_samples_up(obj, group_axis):
+    x_now = lax.all_gather(obj, group_axis)
+    f_next = jnp.concatenate(x_now, 1)
+    return f_next
+
+
+get_corner_in = functools.partial(read_samples_up, group_axis="blk")
 
 
 def layer_norm(values, ln_gain):
@@ -72,7 +82,7 @@
     weight_gate, weight_up, weight_down = (
         lax.all_gather(w_gate, "blk", axis=1, tiled=True),
         lax.all_gather(w_up, "blk", axis=1, tiled=True),
-        lax.all_gather(w_down, "blk", axis=1, tiled=True),
+        get_corner_in(w_down),
     )
     inputs_rows = to_experts(pack_slots(jnp.repeat(normed, top_picks, axis=0)))
     expert_rows, gate_pre, up_pre, hidden_act = expert_forward(

time: 463 us -> 472 us (1.019)
  waiting for transfers between devices: 228 us -> 233 us
    all_gather x1, waiting for transfers between devices: 52.6 us -> 0.01 us  [read_samples_up(): x_now = lax.all_gather(obj, group_axis)]
    all_gather x1, waiting for transfers between devices: 22.6 us -> 52.5 us  [on_device(): lax.all_gather(w_up, 'blk', axis=1, tiled=True)]
    all_gather x1, waiting for transfers between devices: 0.01 us -> 26.9 us  [on_device(): lax.all_gather(w_gate, 'blk', axis=1, tiled=True)]
  transfers between devices with their start and end apart: 10 -> 10, of which waited for: 8 -> 8; matrix products, arithmetic and copies ran while one was open for 36% -> 34% of each run, Pallas kernels for 0% -> 0%
where the time goes in v1:
time: 472 us; the launch traced here: 465 us
  waiting for transfers between devices  233 us (49%)
  local copies, waits for them, and re-layouts  79.7 us (17%)
  matrix products  74.5 us (16%)
  other arithmetic  45.1 us (10%)
  starting transfers between devices  18.2 us (4%)
  between operations  14.6 us (3%)
    reduce_scatter x1, waiting for transfers between devices, on_device(): lax.psum_scatter(grad_down.astype(jnp.bfloat16), 'blk', scatter_dimension...  75.4 us
    all_gather x1, waiting for transfers between devices, on_device(): lax.all_gather(w_up, 'blk', axis=1, tiled=True)  52.5 us
    all_to_all x2, waiting for transfers between devices, to_experts(): lax.all_to_all(packed, 'tile', split_axis=0, concat_axis=2, tiled=True)[0]  30.9 us
    all_to_all x2, waiting for transfers between devices, from_experts(): lax.all_to_all(results[None], 'tile', split_axis=2, concat_axis=0, tiled=...  29.6 us
    all_gather x1, waiting for transfers between devices, on_device(): lax.all_gather(w_gate, 'blk', axis=1, tiled=True)  26.9 us
    gather x2, local copies, waits for them, and re-layouts, from_experts(): picked = returned.reshape(experts_all * capacity, features)[slot_index]  18.1 us
    dot_general x1, matrix products, expert_backward(): jnp.einsum('erd,ehd->erh', d_rows, weight_down, preferred_element_type=jn...  18 us
    reduce_scatter x1, waiting for transfers between devices, on_device(): lax.psum_scatter(grad_up.astype(jnp.bfloat16), 'blk', scatter_dimension=1...  15.3 us
  transfers between devices with their start and end apart: 10, of which 8 were waited for; matrix products, arithmetic and copies ran while one was open for 34% of the time, Pallas kernels for 0%

profile of v1, /device:TPU:0, one launch (start us, length us, event | category | flops | bytes accessed | tf_op | source)
XLA Modules:
  0.0 464.9 jit_solution(13942725846949269249)
XLA Ops:
  20.1 11.5 %scatter_custom_fusion = bf16[3072,384]{1,0:T(8,128)(2,1)} fusion(s32[2048]{0:T(1024)S(1)} %bitcast.77, bf16[2048,384]{1,0:T(8,128)(2,1)} %reshape.161, bf16[]{:T(256)} %constant.10.clone.1), kind=kCustom, calls=%fused_computation.35 | custom fusion | bytes 2359808 | tf_op jit(solution)/shard_map/scatter | solution.py:71
  42.2 5.4 %mul.150 = f32[2048,384]{1,0:T(8,128)} reshape(f32[1024,2,384]{2,1,0:T(2,128)} %mul.146) | data formatting | bytes 6291456 | tf_op jit(solution)/shard_map/mul | solution.py:94
  47.6 12.5 %scatter_custom_fusion.1 = bf16[3072,384]{1,0:T(8,128)(2,1)} fusion(s32[2048]{0:T(1024)S(1)} %bitcast.78, f32[2048,384]{1,0:T(8,128)} %mul.150, f32[2048]{0:T(1024)S(1)} %mul.148, bf16[]{:T(256)} %constant.10.clone.1), kind=kCustom, calls=%fused_computation.32 | custom fusion | flops 1572864 | bytes 5513218 | tf_op jit(solution)/shard_map/scatter | solution.py:71
  72.9 26.3 %all-to-all-done.2 = bf16[4,4,192,384]{3,2,1,0:T(8,128)(2,1)} async-done(((bf16[4,4,192,384]{3,2,1,0:T(8,128)(2,1)}), bf16[4,4,192,384]{3,2,1,0:T(8,128)(2,1)}, u32[]{:S(2)}, u32[]{:S(2)}) %all-to-all-start.2) | async-done | bytes 2359328 | tf_op jit(solution)/shard_map/all_to_all | solution.py:74
  107.0 26.9 %all-gather.5.cloned.1.call-done = bf16[4,384,1024]{2,1,0:T(8,128)(2,1)} async-done(((bf16[4,48,1024]{2,1,0:T(8,128)(2,1)}), bf16[4,384,1024]{2,1,0:T(8,128)(2,1)}) %all-gather.5.cloned.1.call-update) | async-done | bytes 3145744 | tf_op jit(solution)/shard_map/all_gather | solution.py:83
  133.9 8.4 %fusion.21 = f32[4,768,1024]{2,1,0:T(8,128)} fusion(bf16[4,768,384]{2,1,0:T(8,128)(2,1)S(1)} %bitcast.62, bf16[4,384,1024]{2,1,0:T(8,128)(2,1)} %all-gather.5.cloned.1.call-done), kind=kOutput, calls=%fused_computation.53 | convolution fusion | flops 2415919104 | bytes 18087936 | tf_op jit(solution)/shard_map/erd,edh->erh/dot_general | solution.py:25
  142.3 52.5 %all-gather.7.cloned.1.call-done = bf16[4,384,1024]{2,1,0:T(8,128)(2,1)} async-done(((bf16[4,48,1024]{2,1,0:T(8,128)(2,1)}), bf16[4,384,1024]{2,1,0:T(8,128)(2,1)}) %all-gather.7.cloned.1.call-update) | async-done | bytes 3145744 | tf_op jit(solution)/shard_map/all_gather | solution.py:84
  194.8 8.2 %fusion.22 = f32[4,768,1024]{2,1,0:T(8,128)} fusion(bf16[4,768,384]{2,1,0:T(8,128)(2,1)S(1)} %bitcast.63, bf16[4,384,1024]{2,1,0:T(8,128)(2,1)} %all-gather.7.cloned.1.call-done), kind=kOutput, calls=%fused_computation.54 | convolution fusion | flops 2415919104 | bytes 18087936 | tf_op jit(solution)/shard_map/erd,edh->erh/dot_general | solution.py:28
  203.0 18.0 %multiply_convert_fusion = (bf16[4,768,1024]{2,1,0:T(8,128)(2,1)}, bf16[4,768,1024]{2,1,0:T(8,128)(2,1)}, bf16[4,768,1024]{2,1,0:T(8,128)(2,1)}) fusion(f32[4,768,1024]{2,1,0:T(8,128)} %fusion.21, f32[4,768,1024]{2,1,0:T(8,128)} %fusion.22, bf16[4,768,384]{2,1,0:T(8,128)(2,1)} %bitcast.73, bf16[4,1024,384]{2,1,0:T(8,128)(2,1)} %bitcast.71), kind=kOutput, calls=%fused_computation.4 | convolution fusion | flops 2466250752 | bytes 49545216 | tf_op jit(solution)/shard_map/erd,ehd->erh/dot_general | solution.py:40
  221.1 7.1 %convolution_convert_fusion.2 = bf16[4,384,1024]{2,1,0:T(8,128)(2,1)} fusion(bf16[4,768,384]{2,1,0:T(8,128)(2,1)S(1)} %bitcast.64, bf16[4,768,1024]{2,1,0:T(8,128)(2,1)} %get-tuple-element.15), kind=kOutput, calls=%fused_computation.20 | convolution fusion | flops 2417491968 | bytes 11796480 | tf_op jit(solution)/shard_map/erd,erh->edh/dot_general | solution.py:49
  228.7 7.1 %convolution_convert_fusion.1 = bf16[4,384,1024]{2,1,0:T(8,128)(2,1)} fusion(bf16[4,768,384]{2,1,0:T(8,128)(2,1)S(1)} %bitcast.65, bf16[4,768,1024]{2,1,0:T(8,128)(2,1)} %get-tuple-element.14), kind=kOutput, calls=%fused_computation.19 | convolution fusion | flops 2417491968 | bytes 11796480 | tf_op jit(solution)/shard_map/erd,erh->edh/dot_general | solution.py:50
  237.5 8.0 %convolution_convert_fusion = bf16[4,1024,384]{2,1,0:T(8,128)(2,1)} fusion(bf16[4,768,1024]{2,1,0:T(8,128)(2,1)} %get-tuple-element.16, bf16[4,768,384]{2,1,0:T(8,128)(2,1)S(1)} %bitcast.74), kind=kOutput, calls=%fused_computation.18 | convolution fusion | flops 2417491968 | bytes 11796480 | tf_op jit(solution)/shard_map/erh,erd->ehd/dot_general | solution.py:51
  245.5 6.7 %fusion.23 = f32[4,768,384]{2,1,0:T(8,128)S(1)} fusion(bf16[4,768,1024]{2,1,0:T(8,128)(2,1)} %get-tuple-element.15, bf16[4,384,1024]{2,1,0:T(8,128)(2,1)} %all-gather.5.cloned.1.call-done), kind=kOutput, calls=%fused_computation.55 | convolution fusion | flops 2415919104 | bytes 14155776 | tf_op jit(solution)/shard_map/erh,edh->erd/dot_general | solution.py:46
  262.9 7.2 %convert_bitcast_fusion = bf16[1,4,768,384]{3,2,1,0:T(8,128)(2,1)S(1)} fusion(bf16[4,768,1024]{2,1,0:T(8,128)(2,1)} %get-tuple-element.16, bf16[4,1024,384]{2,1,0:T(8,128)(2,1)} %bitcast.72), kind=kOutput, calls=%fused_computation.17 | convolution fusion | flops 2417098752 | bytes 11796480 | tf_op jit(solution)/shard_map/erh,ehd->erd/dot_general | solution.py:31
  273.4 18.0 %all-to-all-done.3 = bf16[1,4,768,384]{3,1,0,2:T(4,128)(2,1)S(1)} async-done(((bf16[1,4,768,384]{3,1,0,2:T(4,128)(2,1)}), bf16[1,4,768,384]{3,1,0,2:T(4,128)(2,1)S(1)}, u32[]{:S(2)}, u32[]{:S(2)}) %all-to-all-start.3) | async-done | bytes 2359328 | tf_op jit(solution)/shard_map/all_to_all | solution.py:78
  300.4 9.0 %gather_fusion.1 = bf16[2048,384]{1,0:T(8,128)(2,1)} fusion(bf16[3072,384]{1,0:T(8,128)(2,1)S(1)} %bitcast.61, s32[2048]{0:T(1024)S(1)} %broadcast_clamp_fusion), kind=kCustom, calls=%fused_computation.1 | custom fusion | bytes 3153920 | tf_op jit(solution)/shard_map/gather | solution.py:79
  309.5 4.9 %reshape.140 = f32[1024,2,384]{2,1,0:T(2,128)} reshape(bf16[2048,384]{1,0:T(8,128)(2,1)} %gather_fusion.1) | data formatting | bytes 4718592 | tf_op jit(solution)/shard_map/convert_element_type | solution.py:80
  314.4 11.6 %all-to-all-done.1 = bf16[1,4,768,384]{3,1,0,2:T(4,128)(2,1)} async-done(((bf16[1,4,768,384]{3,1,0,2:T(4,128)(2,1)}), bf16[1,4,768,384]{3,1,0,2:T(4,128)(2,1)}, u32[]{:S(2)}, u32[]{:S(2)}) %all-to-all-start.1) | async-done | bytes 2359328 | tf_op jit(solution)/shard_map/all_to_all | solution.py:78
  328.1 9.1 %gather_fusion = bf16[2048,384]{1,0:T(8,128)(2,1)} fusion(bf16[3072,384]{1,0:T(8,128)(2,1)S(1)} %bitcast.60, s32[2048]{0:T(1024)S(1)} %broadcast_clamp_fusion), kind=kCustom, calls=%fused_computation | custom fusion | bytes 3153920 | tf_op jit(solution)/shard_map/gather | solution.py:79
  337.2 5.0 %reshape.139 = f32[1024,2,384]{2,1,0:T(2,128)} reshape(bf16[2048,384]{1,0:T(8,128)(2,1)} %gather_fusion) | data formatting | bytes 4718592 | tf_op jit(solution)/shard_map/convert_element_type | solution.py:80
  342.2 10.1 %multiply_reduce_fusion = (f32[1024,2]{1,0:T(8,128)S(1)}, bf16[1024,384]{1,0:T(8,128)(2,1)}) fusion(f32[1024,2,384]{2,1,0:T(2,128)} %reshape.139, f32[1024,384]{1,0:T(8,128)S(1)} %copy-done.4, f32[1024,2]{1,0:T(8,128)S(1)} %copy-done.5), kind=kLoop, calls=%fused_computation.10 | loop fusion | flops 2750464 | bytes 5521408 | tf_op jit(solution)/shard_map/reduce_sum | solution.py:94
  353.1 5.7 %reduce_sum.96 = f32[1024,384]{1,0:T(8,128)S(1)} reduce(f32[1024,2,384]{2,1,0:T(2,128)} %reshape.140, f32[]{:T(128)} %constant.25.clone.1), dimensions={1}, to_apply=%region_9.10 | reduce | flops 393216 | bytes 4718596 | tf_op jit(solution)/shard_map/reduce_sum | solution.py:104
  363.3 15.3 %reduce-scatter.6.cloned.1.call-done = bf16[4,48,1024]{2,1,0:T(8,128)(2,1)} async-done(((bf16[4,384,1024]{2,1,0:T(8,128)(2,1)}), bf16[4,48,1024]{2,1,0:T(8,128)(2,1)}) %reduce-scatter.6.cloned.1.call-update) | async-done | bytes 393232 | tf_op jit(solution)/shard_map/reduce_scatter | solution.py:115
  380.5 75.4 %reduce-scatter.8.cloned.1.call-done = bf16[4,128,384]{2,1,0:T(8,128)(2,1)} async-done(((bf16[4,1024,384]{2,1,0:T(8,128)(2,1)}), bf16[4,128,384]{2,1,0:T(8,128)(2,1)}) %reduce-scatter.8.cloned.1.call-update) | async-done | bytes 393232 | tf_op jit(solution)/shard_map/reduce_scatter | solution.py:118
  (88 shorter events, 80.2 us)
Async XLA Ops:
  7.2 3.7 copy-start.8
  7.2 9.5 %copy-start = (bf16[1024,384]{1,0:T(8,128)(2,1)S(1)}, bf16[1024,384]{1,0:T(8,128)(2,1)}, u32[]{:S(2)}) copy-start(bf16[1024,384]{1,0:T(8,128)(2,1)} %param.8) | copy-start | bytes 2359300
  7.2 95.4 %all-gather.9.cloned.1.call-start = ((), (), s32[]{:S(2)}) async-start(), calls=%async_computation.12 | async-start | bytes 3538944 | tf_op jit(solution)/shard_map/all_gather | solution.py:9
  7.9 126.0 %all-gather.5.cloned.1.call-start = ((), (), s32[]{:S(2)}) async-start(), calls=%async_computation.7 | async-start | bytes 3538944 | tf_op jit(solution)/shard_map/all_gather | solution.py:83
  8.7 186.1 %all-gather.7.cloned.1.call-start = ((), (), s32[]{:S(2)}) async-start(), calls=%async_computation.8 | async-start | bytes 3538944 | tf_op jit(solution)/shard_map/all_gather | solution.py:84
  9.4 7.9 %copy-start.9 = (f32[384]{0:T(512)S(1)}, f32[384]{0:T(512)}, u32[]{:S(2)}) copy-start(f32[384]{0:T(512)} %param.9) | copy-start | bytes 4612
  31.7 4.5 copy-start.10
  31.7 33.1 %all-to-all-start = ((bf16[4,4,192,384]{3,2,1,0:T(8,128)(2,1)}), bf16[4,4,192,384]{3,2,1,0:T(8,128)(2,1)S(1)}, u32[]{:S(2)}, u32[]{:S(2)}) async-start(bf16[4,4,192,384]{3,2,1,0:T(8,128)(2,1)} %bitcast.69), calls=%async_computation | async-start | bytes 4718592 | tf_op jit(solution)/shard_map/all_to_all | solution.py:74
  64.7 1.5 copy-start.1
  66.2 33.0 %all-to-all-start.2 = ((bf16[4,4,192,384]{3,2,1,0:T(8,128)(2,1)}), bf16[4,4,192,384]{3,2,1,0:T(8,128)(2,1)}, u32[]{:S(2)}, u32[]{:S(2)}) async-start(bf16[4,4,192,384]{3,2,1,0:T(8,128)(2,1)} %bitcast.68), calls=%async_computation.2 | async-start | bytes 4718592 | tf_op jit(solution)/shard_map/all_to_all | solution.py:74
  70.7 290.6 %reduce-scatter.4.cloned.1.call-start = ((), (), s32[]{:S(2)}) async-start(), calls=%async_computation.9 | async-start | bytes 3538944 | tf_op jit(solution)/shard_map/reduce_scatter | solution.py:112
  228.2 150.4 %reduce-scatter.6.cloned.1.call-start = ((), (), s32[]{:S(2)}) async-start(), calls=%async_computation.10 | async-start | bytes 3538944 | tf_op jit(solution)/shard_map/reduce_scatter | solution.py:115
  235.8 1.7 copy-start.7
  235.9 220.0 %reduce-scatter.8.cloned.1.call-start = ((), (), s32[]{:S(2)}) async-start(), calls=%async_computation.11 | async-start | bytes 3538944 | tf_op jit(solution)/shard_map/reduce_scatter | solution.py:118
  245.5 6.7 %slice-start = ((s8[6291456]{0:T(1024)(128)(4,1)}), s8[2097152]{0:T(1024)(128)(4,1)S(1)}, s32[]{:S(2)}) async-start(s8[6291456]{0:T(1024)(128)(4,1)} %bitcast.81), calls=%async_computation.13 | async-start | bytes 4194304
  245.5 6.7 %copy-start.6 = (bf16[4,384,1024]{2,1,0:T(8,128)(2,1)S(1)}, bf16[4,384,1024]{2,1,0:T(8,128)(2,1)}, u32[]{:S(2)}) copy-start(bf16[4,384,1024]{2,1,0:T(8,128)(2,1)} %all-gather.7.cloned.1.call-done) | copy-start | bytes 9437188
  245.5 6.8 %slice-start.1 = ((s8[6291456]{0:T(1024)(128)(4,1)}), s8[4194304]{0:T(1024)(128)(4,1)S(1)}, s32[]{:S(2)}) async-start(s8[6291456]{0:T(1024)(128)(4,1)} %bitcast.81), calls=%async_computation.14 | async-start | bytes 8388608
  259.3 32.1 %all-to-all-start.3 = ((bf16[1,4,768,384]{3,1,0,2:T(4,128)(2,1)}), bf16[1,4,768,384]{3,1,0,2:T(4,128)(2,1)S(1)}, u32[]{:S(2)}, u32[]{:S(2)}) async-start(bf16[1,4,768,384]{3,1,0,2:T(4,128)(2,1)} %copy.44), calls=%async_computation.3 | async-start | bytes 4718592 | tf_op jit(solution)/shard_map/all_to_all | solution.py:78
  291.4 1.4 copy-start.2
  292.8 33.2 %all-to-all-start.1 = ((bf16[1,4,768,384]{3,1,0,2:T(4,128)(2,1)}), bf16[1,4,768,384]{3,1,0,2:T(4,128)(2,1)}, u32[]{:S(2)}, u32[]{:S(2)}) async-start(bf16[1,4,768,384]{3,1,0,2:T(4,128)(2,1)} %copy.40), calls=%async_computation.1 | async-start | bytes 4718592 | tf_op jit(solution)/shard_map/all_to_all | solution.py:78
  297.4 2.6 copy-start.3
  337.2 5.0 %copy-start.4 = (f32[1024,384]{1,0:T(8,128)S(1)}, f32[1024,384]{1,0:T(8,128)}, u32[]{:S(2)}) copy-start(f32[1024,384]{1,0:T(8,128)} %convert_element_type.81) | copy-start | bytes 4718596
  337.2 5.0 %copy-start.5 = (f32[1024,2]{1,0:T(8,128)S(1)}, f32[1024,2]{1,0:T(8,128)}, u32[]{:S(2)}) copy-start(f32[1024,2]{1,0:T(8,128)} %copy.34) | copy-start | bytes 24580
Sparse Core Ops, SparseCore 0:
  10.2 62.7 all-gather.8
  75.2 58.6 all-gather.4
  136.1 58.6 all-gather.6
  228.3 73.2 reduce-scatter.3
  305.1 73.4 reduce-scatter.5
  382.0 73.8 reduce-scatter.7
